TPU v7x, 128 devices: a whole 4x4x4 slice. The times are simulated.
128 devices in a mesh: phase: 8 (over y_hi, z), row: 16 (over x, y_lo, core).
Axes of the slice: x: 4, y: 4 (y_hi: 2, y_lo: 2; y = y_hi * 2 + y_lo), z: 4, core: 2. Of those that a mesh axis runs over, the one named last changes fastest.
Arguments:
- frames: float32 [2, 64, 256, 256], P(None, 'phase', 'row'), may hold values from -50 to 50
- auxiliary: float32 [2, 64, 256, 256], P(None, 'phase', 'row'), may hold values from -6 to 6
- scaled_dual: float32 [2, 64, 256, 256], P(None, 'phase', 'row'), may hold values from -3 to 3
- coil_maps: float32 [16, 2, 256, 256], P(None, None, 'row'), may hold values from -5 to 5
- measured: float32 [16, 2, 64, 256, 256], P(None, None, 'phase', 'row'), may hold values from -6 to 6
- sampling: int32 [64, 256], P('phase'), may hold values 0 or 1
Outputs:
- new_frames: float32 [2, 64, 256, 256], P(None, 'phase', 'row')
- new_aux: float32 [2, 64, 256, 256], P(None, 'phase', 'row')
- new_dual: float32 [2, 64, 256, 256], P(None, 'phase', 'row')
- residual_norms: float32 [2], replicated
All inputs are finite; a program needn't handle non-finite values. No bound on the sum of `sampling` on one device may be relied on, other than what follows from the above.
Results may differ from a plain program's by a relative error of at most 0.003.
Values sent between devices are 32-bit elements; how exact they have to be, the bound alone decides.
No kernel may reach another device: no remote copies, remote signals or barrier semaphores. Data moves between devices by JAX's collectives and lax.ppermute only.
A program may use at most 256 MiB of HBM per device.

v0:
```python
import math
import jax
import jax.numpy as jnp
from jax import lax
from jax.sharding import PartitionSpec as P

CG_STEPS = 2
EXACT = lax.Precision.HIGHEST
PENALTY = 0.5
DAMPING = 0.1
THRESHOLD = 1.0


def padded_2(value, sides, width):
    for axis, dim in sides:
        count, length = (lax.axis_size(axis), value.shape[dim])
        up = [(i, (i + 1) % count) for i in range(count)]
        down = [(j, i) for i, j in up]
        last = lax.slice_in_dim(value, length - width, length, axis=dim)
        initial = lax.slice_in_dim(value, 0, width, axis=dim)
        before = lax.ppermute(last, axis, up)
        after = lax.ppermute(initial, axis, down)
        value = jnp.concatenate([before, value, after], axis=dim)
    return value


def from_behind(value, axis, steps):
    count = lax.axis_size(axis)
    pairs = [(source, (source + steps) % count) for source in range(count)]
    return lax.ppermute(value, axis, pairs)


def tables(count):
    indices = jnp.arange(count, dtype=jnp.int32)
    angles = (indices[:, None] * indices[None, :] % count).astype(jnp.float32) * (
        2.0 * math.pi / count
    )
    return (jnp.cos(angles) / math.sqrt(count), jnp.sin(angles) / math.sqrt(count))


def coil_images(maps, values):
    maps_real = maps[:, 0, None]
    maps_imag = maps[:, 1, None]
    return (
        maps_real * values[0] - maps_imag * values[1],
        maps_real * values[1] + maps_imag * values[0],
    )


def coil_combine(maps, real_part, imag_part):
    maps_real = maps[:, 0, None]
    maps_imag = maps[:, 1, None]
    total_real = jnp.sum(maps_real * real_part + maps_imag * imag_part, 0)
    total_imag = jnp.sum(maps_real * imag_part - maps_imag * real_part, 0)
    return jnp.stack([total_real, total_imag], 0)


def second_diff(values):
    padded = padded_2(values, (("phase", 1),), 1)
    return 2.0 * values - padded[:, 2:] - padded[:, :-2]


def residual_energy(residual):
    return lax.psum(jnp.sum(residual * residual), ("phase", "row"))


def conjugate(estimate, rhs, gram_fn):

    def apply_normal(values):
        return gram_fn(values) + PENALTY * second_diff(values) + DAMPING * values

    residual = rhs - apply_normal(estimate)
    direction = residual
    energy = residual_energy(residual)
    for iteration in range(CG_STEPS):
        image_dir = apply_normal(direction)
        curvature = lax.psum(jnp.sum(direction * image_dir), ("phase", "row"))
        step_size = energy / curvature
        estimate = estimate + step_size * direction
        residual = residual - step_size * image_dir
        if iteration + 1 < CG_STEPS:
            fresh = residual_energy(residual)
            direction = residual + fresh / energy * direction
            energy = fresh
    return estimate


def local(frames, auxiliary, scaled_dual, coil_maps, measured, sampling):
    groups = lax.axis_size("row")
    coil_count = coil_maps.shape[0]
    phases = frames.shape[1]
    row_count = frames.shape[2]
    col_count = frames.shape[3]
    row_total = row_count * groups
    narrow = col_count // groups
    cosine, sine_table = tables(row_total)
    weight = sampling.astype(jnp.float32)[:, None, :]

    def apply_table(values, table):
        return jnp.dot(values, table, precision=EXACT)

    def forward(real_part, imag_part):
        return (
            apply_table(real_part, cosine) + apply_table(imag_part, sine_table),
            apply_table(imag_part, cosine) - apply_table(real_part, sine_table),
        )

    def inverse(real_part, imag_part):
        return (
            apply_table(real_part, cosine) - apply_table(imag_part, sine_table),
            apply_table(imag_part, cosine) + apply_table(real_part, sine_table),
        )

    def filtered(real_part, imag_part):
        spec_real, spec_imag = forward(real_part, imag_part)
        return inverse(spec_real * weight, spec_imag * weight)

    def to_columns_layout(values):
        reshaped = values.reshape(values.shape[:-2] + (row_count, groups, narrow))
        return jnp.moveaxis(reshaped, -3, -1)

    difference = auxiliary - scaled_dual
    previous = from_behind(difference[:, -1:], "phase", 1)
    earlier = jnp.concatenate([previous, difference[:, :-1]], 1)
    rhs_penalty = PENALTY * (earlier - difference)
    moved = (
        lax.all_to_all(
            to_columns_layout(frames.reshape(2 * phases, row_count, col_count)),
            "row",
            split_axis=1,
            concat_axis=3,
            tiled=True,
        ),
        lax.all_to_all(
            to_columns_layout(rhs_penalty.reshape(2 * phases, row_count, col_count)),
            "row",
            split_axis=1,
            concat_axis=3,
            tiled=True,
        ),
        lax.all_to_all(
            to_columns_layout(coil_maps.reshape(2 * coil_count, row_count, col_count)),
            "row",
            split_axis=1,
            concat_axis=3,
            tiled=True,
        ),
        lax.all_to_all(
            to_columns_layout(measured.reshape(coil_count * 2 * phases, row_count, col_count)),
            "row",
            split_axis=1,
            concat_axis=3,
            tiled=True,
        ),
    )
    frames_cols = moved[0].reshape(2, phases, narrow, row_total)
    penalty_cols = moved[1].reshape(2, phases, narrow, row_total)
    maps_cols = moved[2].reshape(coil_count, 2, narrow, row_total)
    measured_cols = moved[3].reshape(coil_count, 2, phases, narrow, row_total)

    def gram_columns(values):
        real_part, imag_part = coil_images(maps_cols, values)
        back_real, back_imag = filtered(real_part, imag_part)
        return coil_combine(maps_cols, back_real, back_imag)

    back_real, back_imag = inverse(measured_cols[:, 0] * weight, measured_cols[:, 1] * weight)
    rhs = coil_combine(maps_cols, back_real, back_imag) + penalty_cols
    solved = conjugate(frames_cols, rhs, gram_columns)
    values = solved.reshape(2 * phases, narrow, row_total)
    reshaped = values.reshape(values.shape[:-2] + (narrow, groups, row_count))
    returned = lax.all_to_all(
        jnp.moveaxis(reshaped, -3, -1), "row", split_axis=1, concat_axis=3, tiled=True
    )
    estimate = returned.reshape(2, phases, row_count, col_count)
    following = from_behind(estimate[:, :1], "phase", -1)
    advanced = jnp.concatenate([estimate[:, 1:], following], 1)
    shifted = advanced - estimate + scaled_dual
    magnitude = jnp.sqrt(shifted[0] * shifted[0] + shifted[1] * shifted[1])
    factor = jnp.maximum(magnitude - THRESHOLD, 0.0) / jnp.maximum(magnitude, THRESHOLD)
    new_aux = shifted * factor[None]
    new_dual = shifted - new_aux
    primal_gap = new_dual - scaled_dual
    dual_gap = new_aux - auxiliary
    primal_sum, dual_sum = lax.psum(
        (jnp.sum(primal_gap * primal_gap), jnp.sum(dual_gap * dual_gap)), ("phase", "row")
    )
    residual_norms = jnp.stack([jnp.sqrt(primal_sum), PENALTY * jnp.sqrt(dual_sum)])
    return (estimate, new_aux, new_dual, residual_norms)


def solution(mesh):
    in_specs = (
        P(None, "phase", "row", None),
        P(None, "phase", "row", None),
        P(None, "phase", "row", None),
        P(None, None, "row", None),
        P(None, None, "phase", "row", None),
        P("phase", None),
    )
    out_specs = (
        P(None, "phase", "row", None),
        P(None, "phase", "row", None),
        P(None, "phase", "row", None),
        P(),
    )
    return jax.shard_map(local, mesh=mesh, in_specs=in_specs, out_specs=out_specs, check_vma=False)
```

profile of v0, /device:TPU:1, one launch (start us, length us, event | category | flops | bytes accessed | tf_op | source)
XLA Modules:
  0.0 575.1 jit_solution(8731979419725957966)
XLA Ops:
  4.2 2.9 reshape_reshape.15
  10.5 6.3 %all-to-all-start = ((f32[16,1,4096]{2,1,0:T(1,128)}), f32[16,1,4096]{2,1,0:T(1,128)S(1)}, u32[]{:S(2)}, u32[]{:S(2)}) async-start(f32[16,1,4096]{2,1,0:T(1,128)} %reshape.40), calls=%async_computation | async-start | bytes 524288 | tf_op jit(solution)/shard_map/all_to_all | solution.py:127
  19.5 3.0 reshape.42
  24.2 4.1 all-to-all-start.3
  30.9 4.0 copy.28
  36.7 6.3 %all-to-all-start.1 = ((f32[16,1,8192]{2,1,0:T(1,128)}), f32[16,1,8192]{2,1,0:T(1,128)S(1)}, u32[]{:S(2)}, u32[]{:S(2)}) async-start(f32[16,1,8192]{2,1,0:T(1,128)} %reshape.44), calls=%async_computation.1 | async-start | bytes 1048576 | tf_op jit(solution)/shard_map/all_to_all | solution.py:141
  43.1 19.4 %reshape_reshape.17 = f32[256,16,16,16]{3,2,1,0:T(8,128)} reshape(f32[16,2,8,16,256]{4,3,2,1,0:T(8,128)} %param.10) | data formatting | bytes 8388608 | tf_op jit(solution)/shard_map/reshape;reshape | solution.py:119
  62.5 21.3 %copy.30 = f32[256,16,16,16]{0,3,2,1:T(8,128)} copy(f32[256,16,16,16]{2,1,3,0:T(8,128)} %bitcast.200) | data formatting | bytes 8388608 | tf_op jit(solution)/shard_map/transpose | solution.py:120
  88.5 5.7 all-to-all-start.2
  102.9 4.2 collective-permute-start.1
  120.9 4.4 copy.29
  125.3 3.7 reshape.34
  129.0 2.9 fusion.10
  131.9 2.9 fusion.11
  134.8 3.0 subtract_multiply_fusion.2
  137.8 4.1 fusion.129
  141.9 3.3 add_multiply_fusion.2
  145.3 2.8 fusion.132
  148.1 4.1 convolution_subtract_fusion.2
  152.2 26.4 %copy.31 = f32[256,1,16,16,16]{4,3,2,0,1:T(8,128)} copy(f32[256,1,16,16,16]{0,4,2,3,1:T(8,128)} %bitcast.9) | data formatting | bytes 8388608 | tf_op jit(solution)/shard_map/all_to_all | solution.py:148
  178.6 23.6 %reshape.35 = f32[16,2,8,16,256]{4,3,2,1,0:T(8,128)} reshape(f32[256,1,16,16,16]{4,3,2,0,1:T(8,128)} %copy.31) | data formatting | bytes 8388608 | tf_op jit(solution)/shard_map/reshape | solution.py:159
  202.3 4.6 fusion.14
  206.9 2.9 fusion.16
  209.8 2.9 fusion.25
  212.7 3.0 fusion.22
  215.7 4.3 add_reduce_fusion.2
  220.9 2.9 fusion.7
  223.9 2.9 fusion.6
  226.7 5.1 collective-permute-start.3
  232.3 3.0 add_multiply_fusion.1
  235.3 2.9 fusion.126
  238.2 3.0 subtract_multiply_fusion.1
  241.1 2.9 fusion.123
  244.0 3.1 convolution_subtract_fusion.1
  247.1 3.4 add_reduce_fusion.1
  251.3 67.4 %all-reduce.1 = (f32[]{:T(128)}, f32[]{:T(128)}) all-reduce(f32[]{:T(128)} %get-tuple-element.15, f32[]{:T(128)} %get-tuple-element.14), channel_id=1, replica_groups=mesh['phase'=8,'row'=16] {'phase','row'}, use_global_device_ids=true, to_apply=%region_5.6 | all-reduce | flops 2 | bytes 16 | tf_op jit(solution)/shard_map/psum | solution.py:64
  320.7 62.7 %psum.44 = f32[]{:T(128)} all-reduce(f32[]{:T(128)} %multiply_reduce_fusion.2), channel_id=1, replica_groups=mesh['phase'=8,'row'=16] {'phase','row'}, use_global_device_ids=true, to_apply=%region_11.12 | all-reduce | flops 1 | bytes 8 | tf_op jit(solution)/shard_map/psum | solution.py:64
  384.9 2.9 fusion.3
  387.9 2.9 fusion.2
  394.0 3.0 add_multiply_fusion
  397.0 2.8 fusion.120
  399.8 3.1 subtract_multiply_fusion
  402.9 2.8 fusion.117
  405.7 3.1 convolution_subtract_fusion
  408.8 3.4 add_reduce_fusion
  412.9 66.4 %psum.45 = f32[]{:T(128)} all-reduce(f32[]{:T(128)} %fusion.88), channel_id=1, replica_groups=mesh['phase'=8,'row'=16] {'phase','row'}, use_global_device_ids=true, to_apply=%region_15.16 | all-reduce | flops 1 | bytes 8 | tf_op jit(solution)/shard_map/psum | solution.py:77
  485.8 11.3 %all_to_all.75 = f32[16,1,4096]{2,1,0:T(1,128)S(1)} all-to-all(f32[16,1,4096]{2,1,0:T(1,128)S(1)} %reshape.46), channel_id=1, replica_groups=mesh['phase'=8,'row'=16] {'row'}, dimensions={0} | all-to-all | bytes 524288 | tf_op jit(solution)/shard_map/all_to_all | solution.py:171
  506.9 66.1 %all-reduce = (f32[]{:T(128)}, f32[]{:T(128)}) all-reduce(f32[]{:T(128)} %multiply_reduce_fusion, f32[]{:T(128)} %get-tuple-element.20), channel_id=1, replica_groups=mesh['phase'=8,'row'=16] {'phase','row'}, use_global_device_ids=true, to_apply=%region_19.20 | all-reduce | flops 2 | bytes 16 | tf_op jit(solution)/shard_map/psum | solution.py:184
  (101 shorter events, 64.9 us)
Async XLA Ops:
  1.7 15.1 %collective-permute-start = (f32[2,1,16,256]{3,2,1,0:T(8,128)S(1)}, f32[2,1,16,256]{3,2,1,0:T(8,128)S(1)}, u32[]{:S(2)}, u32[]{:S(2)}) collective-permute-start(f32[2,1,16,256]{3,2,1,0:T(8,128)S(1)} %slice.144), channel_id=1, source_target_pairs={{0,16},{16,32},{32,48},{48,64},{64,80},{80,96},{96,112},{112,0},{1... | collective-permute-start | bytes 98312 | tf_op jit(solution)/shard_map/ppermute | solution.py:30
  10.5 13.7 %all-to-all-start = ((f32[16,1,4096]{2,1,0:T(1,128)}), f32[16,1,4096]{2,1,0:T(1,128)S(1)}, u32[]{:S(2)}, u32[]{:S(2)}) async-start(f32[16,1,4096]{2,1,0:T(1,128)} %reshape.40), calls=%async_computation | async-start | bytes 524288 | tf_op jit(solution)/shard_map/all_to_all | solution.py:127
  19.5 8.8 %copy-start.11 = (f32[16,2,16,256]{3,2,1,0:T(8,128)S(1)}, f32[16,2,16,256]{3,2,1,0:T(8,128)}, u32[]{:S(2)}) copy-start(f32[16,2,16,256]{3,2,1,0:T(8,128)} %param.9) | copy-start | bytes 1572868
  24.2 12.5 %all-to-all-start.3 = ((f32[16,1,4096]{2,1,0:T(1,128)}), f32[16,1,4096]{2,1,0:T(1,128)S(1)}, u32[]{:S(2)}, u32[]{:S(2)}) async-start(f32[16,1,4096]{2,1,0:T(1,128)} %reshape.42), calls=%async_computation.3 | async-start | bytes 524288 | tf_op jit(solution)/shard_map/all_to_all | solution.py:134
  35.0 8.1 %copy-start.12 = (s32[8,256]{1,0:T(8,128)S(1)}, s32[8,256]{1,0:T(8,128)}, u32[]{:S(2)}) copy-start(s32[8,256]{1,0:T(8,128)} %param.11) | copy-start | bytes 24580
  36.7 25.8 %copy-start.8 = (f32[16,1,4096]{2,1,0:T(1,128)}, f32[16,1,4096]{2,1,0:T(1,128)S(1)}, u32[]{:S(2)}) copy-start(f32[16,1,4096]{2,1,0:T(1,128)S(1)} %all-to-all-done.3) | copy-start | bytes 786436
  36.7 51.0 %all-to-all-start.1 = ((f32[16,1,8192]{2,1,0:T(1,128)}), f32[16,1,8192]{2,1,0:T(1,128)S(1)}, u32[]{:S(2)}, u32[]{:S(2)}) async-start(f32[16,1,8192]{2,1,0:T(1,128)} %reshape.44), calls=%async_computation.1 | async-start | bytes 1048576 | tf_op jit(solution)/shard_map/all_to_all | solution.py:141
  87.7 0.8 copy-start.5
  88.5 63.7 %all-to-all-start.2 = ((f32[256,16,16,16]{0,3,2,1:T(8,128)}), f32[256,16,16,16]{0,3,2,1:T(8,128)}, u32[]{:S(2)}, u32[]{:S(2)}) async-start(f32[256,16,16,16]{0,3,2,1:T(8,128)} %copy.30), calls=%async_computation.2 | async-start | bytes 8388608 | tf_op jit(solution)/shard_map/all_to_all | solution.py:148
  101.8 6.5 %copy-start.9 = (f32[16,1,4096]{2,1,0:T(1,128)S(1)}, f32[16,1,4096]{2,1,0:T(1,128)}, u32[]{:S(2)}) copy-start(f32[16,1,4096]{2,1,0:T(1,128)} %copy-done.8) | copy-start | bytes 786436
  102.9 117.1 %collective-permute-start.1 = (f32[2,1,16,256]{3,2,1,0:T(8,128)}, f32[2,1,16,256]{3,2,1,0:T(8,128)}, u32[]{:S(2)}, u32[]{:S(2)}) collective-permute-start(f32[2,1,16,256]{3,2,1,0:T(8,128)} %get-tuple-element.35), channel_id=1, source_target_pairs={{16,0},{32,16},{48,32},{64,48},{80,64},{96,80},{112,96},{0,112},{1... | collective-permute-start | bytes 98312 | tf_op jit(solution)/shard_map/ppermute | solution.py:22
  107.1 112.9 %collective-permute-start.2 = (f32[2,1,16,256]{3,2,1,0:T(8,128)}, f32[2,1,16,256]{3,2,1,0:T(8,128)}, u32[]{:S(2)}, u32[]{:S(2)}) collective-permute-start(f32[2,1,16,256]{3,2,1,0:T(8,128)} %get-tuple-element.36), channel_id=1, source_target_pairs={{0,16},{16,32},{32,48},{48,64},{64,80},{80,96},{96,112},{112,0},{1... | collective-permute-start | bytes 98312 | tf_op jit(solution)/shard_map/ppermute | solution.py:21
  114.1 1.0 copy-start.6
  202.3 4.6 copy-start
  212.7 3.0 copy-start.1
  212.7 3.0 copy-start.2
  226.7 23.8 %collective-permute-start.3 = (f32[2,1,16,256]{3,2,1,0:T(8,128)S(1)}, f32[2,1,16,256]{3,2,1,0:T(8,128)S(1)}, u32[]{:S(2)}, u32[]{:S(2)}) collective-permute-start(f32[2,1,16,256]{3,2,1,0:T(8,128)S(1)} %get-tuple-element.33), channel_id=1, source_target_pairs={{16,0},{32,16},{48,32},{64,48},{80,64},{96,80},{112,96},{0,112},{1... | collective-permute-start | bytes 98312 | tf_op jit(solution)/shard_map/ppermute | solution.py:22
  231.9 18.6 %collective-permute-start.4 = (f32[2,1,16,256]{3,2,1,0:T(8,128)S(1)}, f32[2,1,16,256]{3,2,1,0:T(8,128)S(1)}, u32[]{:S(2)}, u32[]{:S(2)}) collective-permute-start(f32[2,1,16,256]{3,2,1,0:T(8,128)S(1)} %get-tuple-element.34), channel_id=1, source_target_pairs={{0,16},{16,32},{32,48},{48,64},{64,80},{80,96},{96,112},{112,0},{1... | collective-permute-start | bytes 98312 | tf_op jit(solution)/shard_map/ppermute | solution.py:21
  390.8 21.4 %collective-permute-start.5 = (f32[2,1,16,256]{3,2,1,0:T(8,128)S(1)}, f32[2,1,16,256]{3,2,1,0:T(8,128)S(1)}, u32[]{:S(2)}, u32[]{:S(2)}) collective-permute-start(f32[2,1,16,256]{3,2,1,0:T(8,128)S(1)} %get-tuple-element.29), channel_id=1, source_target_pairs={{16,0},{32,16},{48,32},{64,48},{80,64},{96,80},{112,96},{0,112},{1... | collective-permute-start | bytes 98312 | tf_op jit(solution)/shard_map/ppermute | solution.py:22
  393.6 18.7 %collective-permute-start.6 = (f32[2,1,16,256]{3,2,1,0:T(8,128)S(1)}, f32[2,1,16,256]{3,2,1,0:T(8,128)S(1)}, u32[]{:S(2)}, u32[]{:S(2)}) collective-permute-start(f32[2,1,16,256]{3,2,1,0:T(8,128)S(1)} %get-tuple-element.30), channel_id=1, source_target_pairs={{0,16},{16,32},{32,48},{48,64},{64,80},{80,96},{96,112},{112,0},{1... | collective-permute-start | bytes 98312 | tf_op jit(solution)/shard_map/ppermute | solution.py:21
  500.4 4.3 copy-start.4
  501.4 73.5 %copy-start.3 = (f32[2,8,16,256]{3,2,1,0:T(8,128)}, f32[2,8,16,256]{3,2,1,0:T(8,128)S(1)}, u32[]{:S(2)}) copy-start(f32[2,8,16,256]{3,2,1,0:T(8,128)S(1)} %reshape.37) | copy-start | bytes 786436
  501.4 4.8 copy-start.7
  501.4 3.3 collective-permute-start.7
  506.2 68.7 %copy-start.10 = (f32[2,8,16,256]{3,2,1,0:T(8,128)}, f32[2,8,16,256]{3,2,1,0:T(8,128)S(1)}, u32[]{:S(2)}) copy-start(f32[2,8,16,256]{3,2,1,0:T(8,128)S(1)} %get-tuple-element.22) | copy-start | bytes 786436
where the time goes:
time: 583 us; the launch traced here: 575 us
  blocking collectives  274 us (47%)
  local copies, waits for them, and re-layouts  150 us (26%)
  matrix products  88.7 us (15%)
  starting transfers between devices  40.4 us (7%)
  other arithmetic  12.8 us (2%)
  between operations  6.86 us (1%)
    psum x2, blocking collectives, residual_energy(): return lax.psum(jnp.sum(residual * residual), ('phase', 'row'))  130 us
    dot_general x28, matrix products, apply_table(): return jnp.dot(values, table, precision=EXACT)  88.7 us
    psum x1, blocking collectives, conjugate(): curvature = lax.psum(jnp.sum(direction * image_dir), ('phase', 'row'))  66.4 us
    psum x1, blocking collectives, local(): lax.psum((jnp.sum(primal_gap * primal_gap), jnp.sum(dual_gap * dual_gap))...  66.1 us
    transpose x4, local copies, waits for them, and re-layouts, to_columns_layout(): return jnp.moveaxis(reshaped, -3, -1)  29.3 us
    all_to_all x1, local copies, waits for them, and re-layouts, local(): lax.all_to_all(to_columns_layout(measured.reshape(coil_count * 2 * phases...  26.4 us
    another operation x4, local copies, waits for them, and re-layouts, to_columns_layout(): reshaped = values.reshape(values.shape[:-2] + (row_count, groups, narrow))  25.6 us
    reshape x1, local copies, waits for them, and re-layouts, local(): measured_cols = moved[3].reshape(coil_count, 2, phases, narrow, row_total)  23.6 us
  transfers between devices with their start and end apart: 12, of which 2 were waited for; matrix products, arithmetic and copies ran while one was open for 39% of the time, Pallas kernels for 0%

commit v1 on v0

--- a/solution.py
+++ b/solution.py
@@ -3,12 +3,19 @@
 import jax.numpy as jnp
 from jax import lax
 from jax.sharding import PartitionSpec as P
+from jax.lax import psum
 
 CG_STEPS = 2
 EXACT = lax.Precision.HIGHEST
 PENALTY = 0.5
 DAMPING = 0.1
 THRESHOLD = 1.0
+
+
+def lots_all_note(sheet):
+    for idx in ("phase", "row"):
+        sheet = psum(sheet, idx)
+    return sheet
 
 
 def padded_2(value, sides, width):
@@ -181,8 +188,8 @@
     new_dual = shifted - new_aux
     primal_gap = new_dual - scaled_dual
     dual_gap = new_aux - auxiliary
-    primal_sum, dual_sum = lax.psum(
-        (jnp.sum(primal_gap * primal_gap), jnp.sum(dual_gap * dual_gap)), ("phase", "row")
+    primal_sum, dual_sum = lots_all_note(
+        (jnp.sum(primal_gap * primal_gap), jnp.sum(dual_gap * dual_gap))
     )
     residual_norms = jnp.stack([jnp.sqrt(primal_sum), PENALTY * jnp.sqrt(dual_sum)])
     return (estimate, new_aux, new_dual, residual_norms)

time: 583 us -> 571 us (0.979)
  blocking collectives: 274 us -> 262 us
    psum x1 -> x2, blocking collectives: 66.1 us -> 53.9 us  [lots_all_note(): sheet = psum(sheet, idx)]
where the time goes in v1:
time: 571 us; the launch traced here: 563 us
  blocking collectives  262 us (46%)
  local copies, waits for them, and re-layouts  150 us (26%)
  matrix products  88.7 us (16%)
  starting transfers between devices  40.4 us (7%)
  other arithmetic  12.8 us (2%)
  between operations  6.99 us (1%)
    psum x2, blocking collectives, residual_energy(): return lax.psum(jnp.sum(residual * residual), ('phase', 'row'))  130 us
    dot_general x28, matrix products, apply_table(): return jnp.dot(values, table, precision=EXACT)  88.7 us
    psum x1, blocking collectives, conjugate(): curvature = lax.psum(jnp.sum(direction * image_dir), ('phase', 'row'))  66.4 us
    psum x2, blocking collectives, lots_all_note(): sheet = psum(sheet, idx)  53.9 us
    transpose x4, local copies, waits for them, and re-layouts, to_columns_layout(): return jnp.moveaxis(reshaped, -3, -1)  29.3 us
    all_to_all x1, local copies, waits for them, and re-layouts, local(): lax.all_to_all(to_columns_layout(measured.reshape(coil_count * 2 * phases...  26.4 us
    another operation x4, local copies, waits for them, and re-layouts, to_columns_layout(): reshaped = values.reshape(values.shape[:-2] + (row_count, groups, narrow))  25.6 us
    reshape x1, local copies, waits for them, and re-layouts, local(): measured_cols = moved[3].reshape(coil_count, 2, phases, narrow, row_total)  23.6 us
  transfers between devices with their start and end apart: 12, of which 2 were waited for; matrix products, arithmetic and copies ran while one was open for 39% of the time, Pallas kernels for 0%

profile of v1, /device:TPU:1, one launch (start us, length us, event | category | flops | bytes accessed | tf_op | source)
XLA Modules:
  0.0 563.1 jit_solution(15008643688367578190)
XLA Ops:
  4.2 2.9 reshape_reshape.15
  10.5 6.3 %all-to-all-start = ((f32[16,1,4096]{2,1,0:T(1,128)}), f32[16,1,4096]{2,1,0:T(1,128)S(1)}, u32[]{:S(2)}, u32[]{:S(2)}) async-start(f32[16,1,4096]{2,1,0:T(1,128)} %reshape.40), calls=%async_computation | async-start | bytes 524288 | tf_op jit(solution)/shard_map/all_to_all | solution.py:134
  19.5 3.0 reshape.42
  24.2 4.1 all-to-all-start.3
  30.9 4.0 copy.28
  36.7 6.3 %all-to-all-start.1 = ((f32[16,1,8192]{2,1,0:T(1,128)}), f32[16,1,8192]{2,1,0:T(1,128)S(1)}, u32[]{:S(2)}, u32[]{:S(2)}) async-start(f32[16,1,8192]{2,1,0:T(1,128)} %reshape.44), calls=%async_computation.1 | async-start | bytes 1048576 | tf_op jit(solution)/shard_map/all_to_all | solution.py:148
  43.1 19.4 %reshape_reshape.17 = f32[256,16,16,16]{3,2,1,0:T(8,128)} reshape(f32[16,2,8,16,256]{4,3,2,1,0:T(8,128)} %param.10) | data formatting | bytes 8388608 | tf_op jit(solution)/shard_map/reshape;reshape | solution.py:126
  62.5 21.3 %copy.30 = f32[256,16,16,16]{0,3,2,1:T(8,128)} copy(f32[256,16,16,16]{2,1,3,0:T(8,128)} %bitcast.200) | data formatting | bytes 8388608 | tf_op jit(solution)/shard_map/transpose | solution.py:127
  88.5 5.7 %all-to-all-start.2 = ((f32[256,16,16,16]{0,3,2,1:T(8,128)}), f32[256,16,16,16]{0,3,2,1:T(8,128)}, u32[]{:S(2)}, u32[]{:S(2)}) async-start(f32[256,16,16,16]{0,3,2,1:T(8,128)} %copy.30), calls=%async_computation.2 | async-start | bytes 8388608 | tf_op jit(solution)/shard_map/all_to_all | solution.py:155
  102.9 4.2 collective-permute-start.1
  120.9 4.4 copy.29
  125.3 3.7 reshape.34
  129.0 2.9 fusion.10
  131.9 2.9 fusion.11
  134.8 3.0 subtract_multiply_fusion.2
  137.8 4.1 fusion.129
  141.9 3.3 add_multiply_fusion.2
  148.1 4.1 convolution_subtract_fusion.2
  152.2 26.4 %copy.31 = f32[256,1,16,16,16]{4,3,2,0,1:T(8,128)} copy(f32[256,1,16,16,16]{0,4,2,3,1:T(8,128)} %bitcast.9) | data formatting | bytes 8388608 | tf_op jit(solution)/shard_map/all_to_all | solution.py:155
  178.6 23.6 %reshape.35 = f32[16,2,8,16,256]{4,3,2,1,0:T(8,128)} reshape(f32[256,1,16,16,16]{4,3,2,0,1:T(8,128)} %copy.31) | data formatting | bytes 8388608 | tf_op jit(solution)/shard_map/reshape | solution.py:166
  202.3 4.6 fusion.14
  206.9 2.9 fusion.16
  209.8 2.9 fusion.25
  212.7 3.0 fusion.22
  215.7 4.3 add_reduce_fusion.2
  220.9 2.9 fusion.7
  223.9 2.9 fusion.6
  226.7 5.1 collective-permute-start.3
  232.3 3.0 add_multiply_fusion.1
  235.3 2.9 fusion.126
  238.2 3.0 subtract_multiply_fusion.1
  241.1 2.9 fusion.123
  244.0 3.1 convolution_subtract_fusion.1
  247.1 3.4 add_reduce_fusion.1
  251.3 67.4 %all-reduce = (f32[]{:T(128)}, f32[]{:T(128)}) all-reduce(f32[]{:T(128)} %get-tuple-element.15, f32[]{:T(128)} %get-tuple-element.14), channel_id=1, replica_groups=mesh['phase'=8,'row'=16] {'phase','row'}, use_global_device_ids=true, to_apply=%region_5.6 | all-reduce | flops 2 | bytes 16 | tf_op jit(solution)/shard_map/psum | solution.py:71
  320.7 62.7 %psum.58 = f32[]{:T(128)} all-reduce(f32[]{:T(128)} %multiply_reduce_fusion.2), channel_id=1, replica_groups=mesh['phase'=8,'row'=16] {'phase','row'}, use_global_device_ids=true, to_apply=%region_11.12 | all-reduce | flops 1 | bytes 8 | tf_op jit(solution)/shard_map/psum | solution.py:71
  384.9 2.9 fusion.3
  387.9 2.9 fusion.2
  394.0 3.0 add_multiply_fusion
  396.9 2.9 fusion.120
  399.8 3.1 subtract_multiply_fusion
  402.9 2.9 fusion.117
  405.7 3.1 convolution_subtract_fusion
  408.8 3.4 add_reduce_fusion
  412.9 66.4 %psum.59 = f32[]{:T(128)} all-reduce(f32[]{:T(128)} %fusion.88), channel_id=1, replica_groups=mesh['phase'=8,'row'=16] {'phase','row'}, use_global_device_ids=true, to_apply=%region_15.16 | all-reduce | flops 1 | bytes 8 | tf_op jit(solution)/shard_map/psum | solution.py:84
  485.8 11.3 %all_to_all.75 = f32[16,1,4096]{2,1,0:T(1,128)S(1)} all-to-all(f32[16,1,4096]{2,1,0:T(1,128)S(1)} %reshape.46), channel_id=1, replica_groups=mesh['phase'=8,'row'=16] {'row'}, dimensions={0} | all-to-all | bytes 524288 | tf_op jit(solution)/shard_map/all_to_all | solution.py:178
  506.9 21.4 %all-reduce.2 = (f32[]{:T(128)}, f32[]{:T(128)}) all-reduce(f32[]{:T(128)} %multiply_reduce_fusion, f32[]{:T(128)} %get-tuple-element.22), channel_id=1, replica_groups=mesh['phase'=8,'row'=16] {'phase'}, use_global_device_ids=true, to_apply=%region_20.21 | all-reduce | flops 2 | bytes 16 | tf_op jit(solution)/shard_map/psum | solution.py:17
  528.3 32.5 %all-reduce.1 = (f32[]{:T(128)}, f32[]{:T(128)}) all-reduce(f32[]{:T(128)} %get-tuple-element.20, f32[]{:T(128)} %get-tuple-element.21), channel_id=1, replica_groups=mesh['phase'=8,'row'=16] {'row'}, use_global_device_ids=true, to_apply=%region_21.22 | all-reduce | flops 2 | bytes 16 | tf_op jit(solution)/shard_map/psum | solution.py:17
  (102 shorter events, 67.8 us)
Async XLA Ops:
  1.7 15.1 %collective-permute-start = (f32[2,1,16,256]{3,2,1,0:T(8,128)S(1)}, f32[2,1,16,256]{3,2,1,0:T(8,128)S(1)}, u32[]{:S(2)}, u32[]{:S(2)}) collective-permute-start(f32[2,1,16,256]{3,2,1,0:T(8,128)S(1)} %slice.144), channel_id=1, source_target_pairs={{0,16},{16,32},{32,48},{48,64},{64,80},{80,96},{96,112},{112,0},{1... | collective-permute-start | bytes 98312 | tf_op jit(solution)/shard_map/ppermute | solution.py:37
  10.5 13.7 %all-to-all-start = ((f32[16,1,4096]{2,1,0:T(1,128)}), f32[16,1,4096]{2,1,0:T(1,128)S(1)}, u32[]{:S(2)}, u32[]{:S(2)}) async-start(f32[16,1,4096]{2,1,0:T(1,128)} %reshape.40), calls=%async_computation | async-start | bytes 524288 | tf_op jit(solution)/shard_map/all_to_all | solution.py:134
  19.5 8.8 %copy-start.11 = (f32[16,2,16,256]{3,2,1,0:T(8,128)S(1)}, f32[16,2,16,256]{3,2,1,0:T(8,128)}, u32[]{:S(2)}) copy-start(f32[16,2,16,256]{3,2,1,0:T(8,128)} %param.9) | copy-start | bytes 1572868
  24.2 12.5 %all-to-all-start.3 = ((f32[16,1,4096]{2,1,0:T(1,128)}), f32[16,1,4096]{2,1,0:T(1,128)S(1)}, u32[]{:S(2)}, u32[]{:S(2)}) async-start(f32[16,1,4096]{2,1,0:T(1,128)} %reshape.42), calls=%async_computation.3 | async-start | bytes 524288 | tf_op jit(solution)/shard_map/all_to_all | solution.py:141
  35.0 8.1 %copy-start.12 = (s32[8,256]{1,0:T(8,128)S(1)}, s32[8,256]{1,0:T(8,128)}, u32[]{:S(2)}) copy-start(s32[8,256]{1,0:T(8,128)} %param.11) | copy-start | bytes 24580
  36.7 25.8 %copy-start.8 = (f32[16,1,4096]{2,1,0:T(1,128)}, f32[16,1,4096]{2,1,0:T(1,128)S(1)}, u32[]{:S(2)}) copy-start(f32[16,1,4096]{2,1,0:T(1,128)S(1)} %all-to-all-done.3) | copy-start | bytes 786436
  36.7 51.0 %all-to-all-start.1 = ((f32[16,1,8192]{2,1,0:T(1,128)}), f32[16,1,8192]{2,1,0:T(1,128)S(1)}, u32[]{:S(2)}, u32[]{:S(2)}) async-start(f32[16,1,8192]{2,1,0:T(1,128)} %reshape.44), calls=%async_computation.1 | async-start | bytes 1048576 | tf_op jit(solution)/shard_map/all_to_all | solution.py:148
  87.7 0.8 copy-start.5
  88.5 63.7 %all-to-all-start.2 = ((f32[256,16,16,16]{0,3,2,1:T(8,128)}), f32[256,16,16,16]{0,3,2,1:T(8,128)}, u32[]{:S(2)}, u32[]{:S(2)}) async-start(f32[256,16,16,16]{0,3,2,1:T(8,128)} %copy.30), calls=%async_computation.2 | async-start | bytes 8388608 | tf_op jit(solution)/shard_map/all_to_all | solution.py:155
  101.8 6.5 %copy-start.9 = (f32[16,1,4096]{2,1,0:T(1,128)S(1)}, f32[16,1,4096]{2,1,0:T(1,128)}, u32[]{:S(2)}) copy-start(f32[16,1,4096]{2,1,0:T(1,128)} %copy-done.8) | copy-start | bytes 786436
  102.9 117.1 %collective-permute-start.1 = (f32[2,1,16,256]{3,2,1,0:T(8,128)}, f32[2,1,16,256]{3,2,1,0:T(8,128)}, u32[]{:S(2)}, u32[]{:S(2)}) collective-permute-start(f32[2,1,16,256]{3,2,1,0:T(8,128)} %get-tuple-element.37), channel_id=1, source_target_pairs={{16,0},{32,16},{48,32},{64,48},{80,64},{96,80},{112,96},{0,112},{1... | collective-permute-start | bytes 98312 | tf_op jit(solution)/shard_map/ppermute | solution.py:29
  107.1 112.9 %collective-permute-start.2 = (f32[2,1,16,256]{3,2,1,0:T(8,128)}, f32[2,1,16,256]{3,2,1,0:T(8,128)}, u32[]{:S(2)}, u32[]{:S(2)}) collective-permute-start(f32[2,1,16,256]{3,2,1,0:T(8,128)} %get-tuple-element.38), channel_id=1, source_target_pairs={{0,16},{16,32},{32,48},{48,64},{64,80},{80,96},{96,112},{112,0},{1... | collective-permute-start | bytes 98312 | tf_op jit(solution)/shard_map/ppermute | solution.py:28
  114.1 1.0 copy-start.6
  202.3 4.6 copy-start
  212.7 3.0 copy-start.1
  212.7 3.0 copy-start.2
  226.7 23.8 %collective-permute-start.3 = (f32[2,1,16,256]{3,2,1,0:T(8,128)S(1)}, f32[2,1,16,256]{3,2,1,0:T(8,128)S(1)}, u32[]{:S(2)}, u32[]{:S(2)}) collective-permute-start(f32[2,1,16,256]{3,2,1,0:T(8,128)S(1)} %get-tuple-element.35), channel_id=1, source_target_pairs={{16,0},{32,16},{48,32},{64,48},{80,64},{96,80},{112,96},{0,112},{1... | collective-permute-start | bytes 98312 | tf_op jit(solution)/shard_map/ppermute | solution.py:29
  231.9 18.6 %collective-permute-start.4 = (f32[2,1,16,256]{3,2,1,0:T(8,128)S(1)}, f32[2,1,16,256]{3,2,1,0:T(8,128)S(1)}, u32[]{:S(2)}, u32[]{:S(2)}) collective-permute-start(f32[2,1,16,256]{3,2,1,0:T(8,128)S(1)} %get-tuple-element.36), channel_id=1, source_target_pairs={{0,16},{16,32},{32,48},{48,64},{64,80},{80,96},{96,112},{112,0},{1... | collective-permute-start | bytes 98312 | tf_op jit(solution)/shard_map/ppermute | solution.py:28
  390.8 21.5 %collective-permute-start.5 = (f32[2,1,16,256]{3,2,1,0:T(8,128)S(1)}, f32[2,1,16,256]{3,2,1,0:T(8,128)S(1)}, u32[]{:S(2)}, u32[]{:S(2)}) collective-permute-start(f32[2,1,16,256]{3,2,1,0:T(8,128)S(1)} %get-tuple-element.31), channel_id=1, source_target_pairs={{16,0},{32,16},{48,32},{64,48},{80,64},{96,80},{112,96},{0,112},{1... | collective-permute-start | bytes 98312 | tf_op jit(solution)/shard_map/ppermute | solution.py:29
  393.6 18.7 %collective-permute-start.6 = (f32[2,1,16,256]{3,2,1,0:T(8,128)S(1)}, f32[2,1,16,256]{3,2,1,0:T(8,128)S(1)}, u32[]{:S(2)}, u32[]{:S(2)}) collective-permute-start(f32[2,1,16,256]{3,2,1,0:T(8,128)S(1)} %get-tuple-element.32), channel_id=1, source_target_pairs={{0,16},{16,32},{32,48},{48,64},{64,80},{80,96},{96,112},{112,0},{1... | collective-permute-start | bytes 98312 | tf_op jit(solution)/shard_map/ppermute | solution.py:28
  500.4 4.3 copy-start.4
  501.3 61.5 %copy-start.3 = (f32[2,8,16,256]{3,2,1,0:T(8,128)}, f32[2,8,16,256]{3,2,1,0:T(8,128)S(1)}, u32[]{:S(2)}) copy-start(f32[2,8,16,256]{3,2,1,0:T(8,128)S(1)} %reshape.37) | copy-start | bytes 786436
  501.3 4.8 copy-start.7
  501.4 3.3 collective-permute-start.7
  506.2 56.6 %copy-start.10 = (f32[2,8,16,256]{3,2,1,0:T(8,128)}, f32[2,8,16,256]{3,2,1,0:T(8,128)S(1)}, u32[]{:S(2)}) copy-start(f32[2,8,16,256]{3,2,1,0:T(8,128)S(1)} %get-tuple-element.24) | copy-start | bytes 786436
